TPU v7x, 32 devices: a whole 2x2x4 slice. The times are simulated.
32 devices in a mesh: seq: 8 (over z, core), batch: 4 (over y, x).
Axes of the slice: x: 2, y: 2, z: 4, core: 2. Of those that a mesh axis runs over, the one named last changes fastest.
Arguments:
- tokens: bfloat16 [8, 512, 2048], P('batch', 'seq'), may hold values from -6 to 6
- lengths: int32 [8], P('batch'), may hold values from 256 to 512, as said below
- key_mask: int32 [8, 512], P('batch', 'seq'), may hold values 0 or 1
- top_experts: int32 [8, 512, 4], P('batch', 'seq'), may hold values from 0 to 7, all different within a row
- attn_gain: bfloat16 [2048], P(('seq', 'batch')), may hold values from 0.5 to 2
- query_gain: bfloat16 [2048], P(('seq', 'batch')), may hold values from 0.59765625 to 1.59375
- key_gain: bfloat16 [2048], P(('seq', 'batch')), may hold values from 0.59765625 to 1.59375
- mlp_gain: bfloat16 [2048], P(('seq', 'batch')), may hold values from 0.5 to 2
- w_query: bfloat16 [2048, 2048], P(('seq', 'batch')), may hold values from -0.125 to 0.125
- w_key: bfloat16 [2048, 2048], P(('seq', 'batch')), may hold values from -0.125 to 0.125
- w_value: bfloat16 [2048, 2048], P(('seq', 'batch')), may hold values from -0.125 to 0.125
- w_out: bfloat16 [2048, 2048], P(('seq', 'batch')), may hold values from -1 to 1
- w_router: bfloat16 [2048, 8], P(('seq', 'batch')), may hold values from -0.0625 to 0.0625
- expert_gate: bfloat16 [8, 2048, 1024], P('batch', 'seq'), may hold values from -0.125 to 0.125
- expert_up: bfloat16 [8, 2048, 1024], P('batch', 'seq'), may hold values from -0.125 to 0.125
- expert_down: bfloat16 [8, 1024, 2048], P('batch', 'seq'), may hold values from -1 to 1
- cotangent: bfloat16 [8, 512, 2048], P('batch', 'seq'), may hold values from -6 to 6
Outputs:
- output: bfloat16 [8, 512, 2048], P('batch', 'seq')
- grad_tokens: bfloat16 [8, 512, 2048], P('batch', 'seq')
- grad_attn_gain: float32 [2048], P(('seq', 'batch'))
- grad_query_gain: float32 [2048], P(('seq', 'batch'))
- grad_key_gain: float32 [2048], P(('seq', 'batch'))
- grad_mlp_gain: float32 [2048], P(('seq', 'batch'))
- grad_query: float32 [2048, 2048], P(('seq', 'batch'))
- grad_key: float32 [2048, 2048], P(('seq', 'batch'))
- grad_value: float32 [2048, 2048], P(('seq', 'batch'))
- grad_out: float32 [2048, 2048], P(('seq', 'batch'))
- grad_router: float32 [2048, 8], P(('seq', 'batch'))
- grad_expert_gate: float32 [8, 2048, 1024], P('batch', 'seq')
- grad_expert_up: float32 [8, 2048, 1024], P('batch', 'seq')
- grad_expert_down: float32 [8, 1024, 2048], P('batch', 'seq')
Inputs may be any that keep to these rules, and one draw needn't show every extreme that they name: `lengths`: positions at or past a row's length are padding; some row of every draw is full. `top_experts`: each token names 4 different experts.
All inputs are finite; a program needn't handle non-finite values. No bound on the sum of `key_mask` on one device may be relied on, other than what follows from the above.
Results may differ from a plain program's by a relative error of at most 0.038.
Values may be sent and summed in bfloat16 or wider, within the bound.
A program may use at most 320 MiB of HBM per device.

v0:
```python
import jax
import jax.numpy as jnp
from jax import lax
from jax.sharding import PartitionSpec as P

HEAD = 128
EPS = 1e-05
HIGHEST = lax.Precision.HIGHEST
NEGATIVE = -1e30
BF = jnp.bfloat16
F32 = jnp.float32


def dot(a, b):
    return jnp.dot(a, b, preferred_element_type=F32)


def dot_t(a, b):
    return lax.dot_general(a, b, (((1,), (1,)), ((), ())), preferred_element_type=F32)


def t_dot(a, b):
    return lax.dot_general(a, b, (((0,), (0,)), ((), ())), preferred_element_type=F32)


def rms_scale(v):
    return lax.rsqrt(jnp.mean(v * v, axis=-1, keepdims=True) + EPS)


def rms_back(v, scale, gain, grad):
    normal = v * scale
    weighted = grad * gain
    mean = jnp.mean(weighted * normal, axis=-1, keepdims=True)
    return (scale * (weighted - normal * mean), grad * normal)


def rotary_tables(positions):
    half_head = HEAD // 2
    frequency = 10000.0 ** (-2.0 * jnp.arange(half_head, dtype=F32) / HEAD)
    angles = positions.astype(F32)[:, None] * frequency[None, :]
    return (jnp.cos(angles), jnp.sin(angles))


def rotate(v, cos_part, sin_part):
    first, second = jnp.split(v, 2, axis=-1)
    return jnp.concatenate(
        [first * cos_part - second * sin_part, second * cos_part + first * sin_part], axis=-1
    )


def shards(
    tokens,
    lengths,
    key_mask,
    top_experts,
    attn_gain,
    query_gain,
    key_gain,
    mlp_gain,
    w_query,
    w_key,
    w_value,
    w_out,
    w_router,
    expert_gate,
    expert_up,
    expert_down,
    cotangent,
):
    n_seq = lax.axis_size("seq")
    n_bat = lax.axis_size("batch")
    seq = lax.axis_index("seq")
    bat = lax.axis_index("batch")
    rows, span, dim = tokens.shape
    own = rows * span
    col = n_seq * own
    length = n_seq * span
    shard = w_query.shape[0]
    wide = dim // n_seq
    heads = wide // HEAD
    local_experts, depth, hidden_units = expert_gate.shape
    part = hidden_units // n_seq
    experts = local_experts * n_bat
    every = ("seq", "batch")
    score_scale = HEAD ** (-0.5)
    small = jnp.concatenate(
        [w_router, jnp.stack([attn_gain, query_gain, key_gain, mlp_gain], axis=1)], axis=1
    )
    small_all = lax.all_gather(small, every, axis=0, tiled=True)
    router = small_all[:, :experts]
    gain_attn = small_all[:, experts].astype(F32)
    gain_mlp = small_all[:, experts + 3].astype(F32)
    gain_q = lax.dynamic_slice_in_dim(small_all[:, experts + 1], seq * wide, wide).astype(F32)
    gain_k = lax.dynamic_slice_in_dim(small_all[:, experts + 2], seq * wide, wide).astype(F32)
    qkv_cut = jnp.stack([w_query, w_key, w_value]).reshape(3, shard, n_seq, wide)
    qkv_cut = jnp.transpose(qkv_cut, (2, 1, 0, 3)).reshape(n_seq, shard, 3 * wide)
    qkv_cut = lax.all_to_all(qkv_cut, "seq", 0, 0, tiled=True)
    w_qkv = lax.all_gather(qkv_cut, "batch", axis=1, tiled=True).reshape(dim, 3 * wide)
    w_o = lax.all_gather(w_out, "batch", axis=0, tiled=True)
    gu_cut = jnp.stack([expert_gate, expert_up]).reshape(2, local_experts, depth, n_seq, part)
    gu_cut = jnp.transpose(gu_cut, (3, 2, 0, 1, 4)).reshape(n_seq, depth, 2 * local_experts * part)
    w_gu = lax.all_to_all(gu_cut, "seq", 0, 0, tiled=True).reshape(dim, 2 * local_experts * part)
    w_down = expert_down.reshape(local_experts * part, dim)
    mine = tokens.reshape(own, dim)
    x_col = lax.all_gather(mine, "seq", axis=0, tiled=True).astype(F32)
    scale_x = rms_scale(x_col)
    hidden = (x_col * scale_x * gain_attn).astype(BF)
    qkv = dot(hidden, w_qkv)
    q_pre, k_pre, v_pre = (qkv[:, :wide], qkv[:, wide : 2 * wide], qkv[:, 2 * wide :])
    squares = jnp.stack([jnp.sum(q_pre * q_pre, axis=-1), jnp.sum(k_pre * k_pre, axis=-1)])
    squares = lax.psum(squares, "seq")
    scales = lax.rsqrt(squares / dim + EPS)
    scale_q, scale_k = (scales[0][:, None], scales[1][:, None])

    def by_row(v):
        v = v.reshape(n_seq, rows, span, heads, HEAD)
        return jnp.transpose(v, (1, 3, 0, 2, 4)).reshape(rows, heads, length, HEAD)

    def by_col(v):
        v = v.reshape(rows, heads, n_seq, span, HEAD)
        return jnp.transpose(v, (2, 0, 3, 1, 4)).reshape(col, wide)

    positions = jnp.arange(length, dtype=jnp.int32)
    cos_part, sin_part = rotary_tables(positions)
    q_norm = by_row(q_pre * scale_q)
    k_norm = by_row(k_pre * scale_k)
    gain_qh = gain_q.reshape(1, heads, 1, HEAD)
    gain_kh = gain_k.reshape(1, heads, 1, HEAD)
    queries = rotate(q_norm * gain_qh, cos_part, sin_part).astype(BF)
    keys = rotate(k_norm * gain_kh, cos_part, sin_part).astype(BF)
    values = by_row(v_pre.astype(BF))
    mask_all = lax.all_gather(key_mask, "seq", axis=1, tiled=True)
    usable = (positions[None, :] < lengths[:, None]) & (mask_all == 1)
    causal = positions[None, :] <= positions[:, None]
    same = positions[None, :] == positions[:, None]
    allowed = (causal[None] & (usable[:, None, :] | same[None]))[:, None]
    scores = jnp.einsum("rhqd,rhkd->rhqk", queries, keys, preferred_element_type=F32) * score_scale
    scores = jnp.where(allowed, scores, NEGATIVE)
    top = jnp.max(scores, axis=-1, keepdims=True)
    raised = jnp.exp(scores - top)
    probs = raised / jnp.sum(raised, axis=-1, keepdims=True)
    probs_low = probs.astype(BF)
    attended = jnp.einsum("rhqk,rhkd->rhqd", probs_low, values, preferred_element_type=F32)
    mixed = by_col(attended.astype(BF))
    mixed_out = lax.psum_scatter(dot(mixed, w_o).astype(BF), "seq", scatter_dimension=0, tiled=True)
    x_own = mine.astype(F32)
    residual = x_own + mixed_out.astype(F32)
    scale_r = rms_scale(residual)
    normed = (residual * scale_r * gain_mlp).astype(BF)
    router_probs = jax.nn.softmax(dot(normed, router), axis=-1)
    expert_ids = jnp.arange(experts, dtype=jnp.int32)
    chosen = jnp.any(top_experts.reshape(own, -1)[:, :, None] == expert_ids, axis=1).astype(F32)
    gates = router_probs * chosen
    normed_all = lax.all_gather(normed, every, axis=0, tiled=True)
    gates_all = lax.all_gather(gates, every, axis=0, tiled=True)
    dy_own = cotangent.reshape(own, dim)
    dy_all = lax.all_gather(dy_own, every, axis=0, tiled=True)
    first_expert = bat * local_experts
    gates_here = lax.dynamic_slice_in_dim(gates_all, first_expert, local_experts, 1)
    units = local_experts * part
    gates_wide = jnp.repeat(gates_here, part, axis=1)
    pre = dot(normed_all, w_gu)
    gate_pre, up_pre = (pre[:, :units], pre[:, units:])
    sig = jax.nn.sigmoid(gate_pre)
    silu = gate_pre * sig
    active = (silu * up_pre).astype(BF).astype(F32)
    weighted = (active * gates_wide).astype(BF)
    mixture = dot(weighted, w_down).astype(BF)
    mixture = lax.psum_scatter(mixture, every, scatter_dimension=0, tiled=True)
    output = (residual + mixture.astype(F32)).astype(BF)
    back = dot_t(dy_all, w_down)
    gate_terms = jnp.sum((active * back).reshape(-1, local_experts, part), axis=-1)
    grad_active = back * gates_wide
    grad_gate_pre = (grad_active * up_pre * sig * (1.0 + gate_pre * (1.0 - sig))).astype(BF)
    grad_up_pre = (grad_active * silu).astype(BF)
    grad_pre = jnp.concatenate([grad_gate_pre, grad_up_pre], axis=1)
    grad_down = t_dot(weighted, dy_all)
    grad_gu = t_dot(normed_all, grad_pre).astype(BF)
    grad_normed = dot_t(grad_pre, w_gu).astype(BF)
    grad_normed = lax.psum_scatter(grad_normed, every, scatter_dimension=0, tiled=True).astype(F32)
    grad_gates = lax.dynamic_update_slice_in_dim(
        jnp.zeros((normed_all.shape[0], experts), F32), gate_terms, first_expert, 1
    )
    grad_gates = lax.psum_scatter(grad_gates, every, scatter_dimension=0, tiled=True)
    grad_gu = lax.all_to_all(grad_gu.reshape(n_seq, depth, -1), "seq", 0, 0, tiled=True)
    grad_gu = grad_gu.reshape(n_seq, depth, 2, local_experts, part)
    grad_gu = jnp.transpose(grad_gu, (2, 3, 1, 0, 4)).reshape(2, local_experts, depth, hidden_units)
    grad_gu = grad_gu.astype(F32)
    grad_down = grad_down.reshape(local_experts, part, dim)
    grad_chosen = grad_gates * chosen
    grad_logits = router_probs * (
        grad_chosen - jnp.sum(router_probs * grad_chosen, axis=-1, keepdims=True)
    )
    grad_router = lax.dot_general(
        normed.astype(F32), grad_logits, (((0,), (0,)), ((), ())), precision=HIGHEST
    )
    grad_normed = grad_normed + lax.dot_general(
        grad_logits, router.astype(F32), (((1,), (1,)), ((), ())), precision=HIGHEST
    )
    grad_resid, gain_mlp_terms = rms_back(residual, scale_r, gain_mlp, grad_normed)
    grad_residual = dy_own.astype(F32) + grad_resid
    grad_o = grad_residual.astype(BF)
    grad_o_col = lax.all_gather(grad_o, "seq", axis=0, tiled=True)
    grad_mixed = by_row(dot_t(grad_o_col, w_o).astype(BF))
    grad_w_o = t_dot(mixed, grad_o_col).astype(BF)
    grad_w_o = lax.psum_scatter(grad_w_o, "batch", scatter_dimension=0, tiled=True).astype(F32)
    row_dot = jnp.sum(grad_mixed.astype(F32) * attended, axis=-1, keepdims=True)
    grad_values = jnp.einsum("rhqk,rhqd->rhkd", probs_low, grad_mixed, preferred_element_type=F32)
    grad_probs = jnp.einsum("rhqd,rhkd->rhqk", grad_mixed, values, preferred_element_type=F32)
    grad_scores = (probs * (grad_probs - row_dot)).astype(BF)
    grad_q = score_scale * jnp.einsum(
        "rhqk,rhkd->rhqd", grad_scores, keys, preferred_element_type=F32
    )
    grad_k = score_scale * jnp.einsum(
        "rhqk,rhqd->rhkd", grad_scores, queries, preferred_element_type=F32
    )
    grad_q = rotate(grad_q, cos_part, -sin_part)
    grad_k = rotate(grad_k, cos_part, -sin_part)
    grad_gain_q = jnp.sum(grad_q * q_norm, axis=(0, 2)).reshape(wide)
    grad_gain_k = jnp.sum(grad_k * k_norm, axis=(0, 2)).reshape(wide)
    q_weighted = by_col(grad_q * gain_qh)
    k_weighted = by_col(grad_k * gain_kh)
    q_flat = q_pre * scale_q
    k_flat = k_pre * scale_k
    means = jnp.stack(
        [jnp.sum(q_weighted * q_flat, axis=-1), jnp.sum(k_weighted * k_flat, axis=-1)]
    )
    means = lax.psum(means, "seq") / dim
    grad_q_pre = (scale_q * (q_weighted - q_flat * means[0][:, None])).astype(BF)
    grad_k_pre = (scale_k * (k_weighted - k_flat * means[1][:, None])).astype(BF)
    grad_qkv = jnp.concatenate([grad_q_pre, grad_k_pre, by_col(grad_values).astype(BF)], axis=1)
    grad_hidden = dot_t(grad_qkv, w_qkv).astype(BF)
    grad_hidden = lax.psum_scatter(grad_hidden, "seq", scatter_dimension=0, tiled=True).astype(F32)
    grad_w = t_dot(hidden, grad_qkv).astype(BF).reshape(n_seq, n_bat * shard, 3 * wide)
    grad_w = lax.psum_scatter(grad_w, "batch", scatter_dimension=1, tiled=True)
    grad_w = lax.all_to_all(grad_w, "seq", 0, 0, tiled=True).astype(F32)
    grad_w = grad_w.reshape(n_seq, shard, 3, wide)
    grad_w = jnp.transpose(grad_w, (2, 1, 0, 3)).reshape(3, shard, dim)
    grad_x, gain_attn_terms = rms_back(x_own, rms_scale(x_own), gain_attn, grad_hidden)
    grad_tokens = (grad_residual + grad_x).astype(BF)
    zeros = jnp.zeros((dim,), F32)
    small_grads = jnp.concatenate(
        [
            grad_router,
            jnp.stack(
                [
                    jnp.sum(gain_attn_terms, axis=0),
                    lax.dynamic_update_slice_in_dim(zeros, grad_gain_q, seq * wide, 0),
                    lax.dynamic_update_slice_in_dim(zeros, grad_gain_k, seq * wide, 0),
                    jnp.sum(gain_mlp_terms, axis=0),
                ],
                axis=1,
            ),
        ],
        axis=1,
    )
    small_grads = lax.psum_scatter(small_grads, every, scatter_dimension=0, tiled=True)
    return (
        output.reshape(rows, span, dim),
        grad_tokens.reshape(rows, span, dim),
        small_grads[:, experts],
        small_grads[:, experts + 1],
        small_grads[:, experts + 2],
        small_grads[:, experts + 3],
        grad_w[0],
        grad_w[1],
        grad_w[2],
        grad_w_o,
        small_grads[:, :experts],
        grad_gu[0],
        grad_gu[1],
        grad_down,
    )


def solution(mesh):
    tok = P("batch", "seq", None)
    vec = P(("seq", "batch"))
    mat = P(("seq", "batch"), None)
    in_specs = (tok, P("batch"), P("batch", "seq"), tok) + (vec,) * 4 + (mat,) * 5 + (tok,) * 4
    out_specs = (tok, tok) + (vec,) * 4 + (mat,) * 5 + (tok,) * 3
    return jax.shard_map(shards, mesh=mesh, in_specs=in_specs, out_specs=out_specs, check_vma=False)
```

profile of v0, /device:TPU:0, one launch (start us, length us, event | category | flops | bytes accessed | tf_op | source)
XLA Modules:
  0.0 1895.5 jit_solution(7305523587902170462)
XLA Ops:
  15.1 47.5 %all_to_all.20 = bf16[8,64,768]{2,1,0:T(8,128)(2,1)} all-to-all(bf16[8,64,768]{2,1,0:T(8,128)(2,1)S(1)} %reshape.364), channel_id=1, replica_groups=mesh['seq'=8,'batch'=4] {'seq'}, dimensions={0} | all-to-all | bytes 1572864 | tf_op jit(solution)/shard_map/all_to_all | solution.py:97
  63.6 10.6 all-gather
  74.4 66.6 %all-gather.1 = bf16[32,64,12]{1,2,0:T(8,128)(2,1)S(1)} all-gather(bf16[1,64,12]{1,2,0:T(8,128)(2,1)S(1)} %bitcast.250), channel_id=1, replica_groups=mesh['seq'=8,'batch'=4] {'seq','batch'}, dimensions={0}, use_global_device_ids=true | all-gather | bytes 50688 | tf_op jit(solution)/shard_map/all_gather | solution.py:89
  144.3 3.1 fusion.1
  147.4 6.7 fusion.15
  155.8 14.1 psum.14
  170.5 3.0 slice_multiply_fusion.1
  173.5 2.5 copy.211
  176.0 2.7 reshape.366
  178.7 2.3 copy.212
  182.4 2.7 reshape.368
  187.9 1.9 subtract_convert_fusion.1
  189.9 5.8 fusion.55
  195.6 2.8 fusion.10
  202.2 4.6 convolution_convert_fusion.2
  206.9 46.3 %reduce-scatter.11.cloned.1.call-done = bf16[128,2048]{1,0:T(8,128)(2,1)} async-done(((bf16[1024,2048]{1,0:T(8,128)(2,1)}), bf16[128,2048]{1,0:T(8,128)(2,1)}) %reduce-scatter.11.cloned.1.call-update) | async-done | bytes 524304 | tf_op jit(solution)/shard_map/reduce_scatter | solution.py:145
  254.5 2.0 multiply_convert_fusion.6
  257.2 2.3 copy.219
  259.4 2.3 copy.220
  261.7 1.9 maximum_bitcast_fusion
  265.0 4.3 all-to-all-start.1
  270.3 76.5 %all-to-all-done.1 = bf16[8,256,512]{1,2,0:T(8,128)(2,1)} async-done(((bf16[8,256,512]{1,2,0:T(8,128)(2,1)}), bf16[8,256,512]{1,2,0:T(8,128)(2,1)}, u32[]{:S(2)}, u32[]{:S(2)}) %all-to-all-start.1) | async-done | bytes 2097184 | tf_op jit(solution)/shard_map/all_to_all | solution.py:102
  346.8 3.9 copy.222
  350.7 52.5 %all-gather.15.cloned.1.call-done = bf16[4096,2048]{1,0:T(8,128)(2,1)} async-done(((bf16[128,2048]{1,0:T(8,128)(2,1)}), bf16[4096,2048]{1,0:T(8,128)(2,1)}) %all-gather.15.cloned.1.call-update) | async-done | bytes 16777232 | tf_op jit(solution)/shard_map/all_gather | solution.py:154
  403.2 15.1 fusion.58
  418.3 100.7 %all-gather.17.cloned.1.call-done = bf16[4096,2048]{1,0:T(8,128)(2,1)} async-done(((bf16[128,2048]{1,0:T(8,128)(2,1)}), bf16[4096,2048]{1,0:T(8,128)(2,1)}) %all-gather.17.cloned.1.call-update) | async-done | bytes 16777232 | tf_op jit(solution)/shard_map/all_gather | solution.py:157
  519.0 20.0 %bitcast_reduce_fusion = (f32[4096,2]{0,1:T(2,128)S(1)}, bf16[4096,256]{0,1:T(8,128)(2,1)}, f32[4096,256]{0,1:T(8,128)}) fusion(f32[4096,512]{0,1:T(8,128)} %fusion.58, bf16[4096,2048]{1,0:T(8,128)(2,1)} %all-gather.17.cloned.1.call-done, bf16[256,2048]{1,0:T(8,128)(2,1)S(1)} %bitcast.183), kind=kOutput, calls=%fused_computation.13 | convolution fusion | flops 4304396288 | bytes 32538624 | tf_op jit(solution)/shard_map/dot_general | solution.py:19
  540.8 131.0 %reduce-scatter.17.cloned.1.call-done = f32[128,8]{0,1:T(8,128)} async-done(((f32[4096,8]{0,1:T(8,128)}), f32[128,8]{0,1:T(8,128)}) %reduce-scatter.17.cloned.1.call-update) | async-done | bytes 4112 | tf_op jit(solution)/shard_map/reduce_scatter | solution.py:184
  672.6 64.6 %all_gather.33 = f32[4096,8]{0,1:T(8,128)S(1)} all-gather(f32[128,8]{0,1:T(8,128)S(1)} %get-tuple-element.63), channel_id=1, replica_groups=mesh['seq'=8,'batch'=4] {'seq','batch'}, dimensions={0}, use_global_device_ids=true | all-gather | bytes 135168 | tf_op jit(solution)/shard_map/all_gather | solution.py:155
  737.2 7.3 multiply_convert_fusion.2
  746.6 14.1 convolution_convert_fusion
  760.7 355.7 %reduce-scatter.15.cloned.1.call-done = bf16[128,2048]{1,0:T(8,128)(2,1)} async-done(((bf16[4096,2048]{1,0:T(8,128)(2,1)}), bf16[128,2048]{1,0:T(8,128)(2,1)}) %reduce-scatter.15.cloned.1.call-update) | async-done | bytes 524304 | tf_op jit(solution)/shard_map/reduce_scatter | solution.py:180
  1116.5 2.3 multiply_reduce_fusion
  1119.7 2.5 fusion.49
  1122.5 48.6 %all-gather.19.cloned.1.call-done = bf16[1024,2048]{1,0:T(8,128)(2,1)} async-done(((bf16[128,2048]{1,0:T(8,128)(2,1)}), bf16[1024,2048]{1,0:T(8,128)(2,1)}) %all-gather.19.cloned.1.call-update) | async-done | bytes 4194320 | tf_op jit(solution)/shard_map/all_gather | solution.py:203
  1171.0 4.6 convolution_convert_fusion.8
  1175.6 2.0 reshape.381
  1180.7 2.3 convolution_convert_fusion.7
  1186.1 2.0 convolution_multiply_fusion.1
  1189.5 2.0 copy.241
  1191.6 4.3 multiply_subtract_fusion.1
  1200.0 2.5 copy.238
  1204.3 2.0 copy.236
  1209.9 2.5 copy.237
  1213.8 14.8 psum.15
  1228.7 1.9 multiply_convert_fusion.5
  1232.4 5.5 convolution_convert_fusion.4
  1238.0 4.5 convolution_convert_fusion.6
  1242.6 7.8 convolution_convert_fusion.3
  1250.9 9.9 convolution_convert_fusion.1
  1260.7 14.7 convolution_convert_fusion.5
  1275.5 4.4 all-to-all-start.3
  1280.1 59.8 %all-to-all-done.3 = bf16[8,256,512]{2,1,0:T(8,128)(2,1)} async-done(((bf16[8,256,512]{2,1,0:T(8,128)(2,1)}), bf16[8,256,512]{2,1,0:T(8,128)(2,1)}, u32[]{:S(2)}, u32[]{:S(2)}) %all-to-all-start.3) | async-done | bytes 2097184 | tf_op jit(solution)/shard_map/all_to_all | solution.py:185
  1339.9 3.5 all-to-all-start.2
  1343.6 12.4 fusion.59
  1356.2 5.6 reshape.395
  1361.8 4.6 copy.284
  1366.5 2.4 fusion.50
  1368.8 2.7 squeeze.39
  1371.5 2.7 squeeze.38
  1379.2 4.6 fusion.51
  1390.5 354.9 %reduce-scatter.13.cloned.1.call-done = bf16[128,2048]{1,0:T(8,128)(2,1)} async-done(((bf16[4096,2048]{1,0:T(8,128)(2,1)}), bf16[128,2048]{1,0:T(8,128)(2,1)}) %reduce-scatter.13.cloned.1.call-update) | async-done | bytes 524304 | tf_op jit(solution)/shard_map/reduce_scatter | solution.py:169
  1745.5 3.3 fusion.19
  1748.8 135.2 %reduce-scatter.25.cloned.1.call-done = f32[64,12]{1,0:T(8,128)} async-done(((f32[2048,12]{1,0:T(8,128)}), f32[64,12]{1,0:T(8,128)}) %reduce-scatter.25.cloned.1.call-update) | async-done | bytes 3088
  (245 shorter events, 70.0 us)
Async XLA Ops:
  7.2 511.8 %copy-start = (bf16[2,128,2048]{2,1,0:T(8,128)(2,1)S(1)}, bf16[2,128,2048]{2,1,0:T(8,128)(2,1)}, u32[]{:S(2)}) copy-start(bf16[2,128,2048]{2,1,0:T(8,128)(2,1)} %param.32) | copy-start | bytes 3145732
  7.2 137.1 %all-gather.9.cloned.1.call-start = ((), (), s32[]{:S(2)}) async-start(), calls=%async_computation.12 | async-start | bytes 4718592 | tf_op jit(solution)/shard_map/all_gather | solution.py:105
  7.9 139.5 %all-gather.11.cloned.1.call-start = ((), (), s32[]{:S(2)}) async-start(), calls=%async_computation.13 | async-start | bytes 3932160 | tf_op jit(solution)/shard_map/all_gather | solution.py:98
  11.8 51.8 %copy-start.52 = (s32[2,64]{1,0:T(2,128)S(1)}, s32[2,64]{1,0:T(2,128)}, u32[]{:S(2)}) copy-start(s32[2,64]{1,0:T(2,128)} %param.19) | copy-start | bytes 1540
  11.8 62.5 %copy-start.49 = (bf16[64,8]{0,1:T(8,128)(2,1)S(1)}, bf16[64,8]{0,1:T(8,128)(2,1)}, u32[]{:S(2)}) copy-start(bf16[64,8]{0,1:T(8,128)(2,1)} %param.29) | copy-start | bytes 3076
  11.8 62.4 %copy-start.53 = (bf16[64]{0:T(256)(128)(2,1)S(1)}, bf16[64]{0:T(256)(128)(2,1)}, u32[]{:S(2)}) copy-start(bf16[64]{0:T(256)(128)(2,1)} %param.21) | copy-start | bytes 388
  11.9 62.4 %copy-start.54 = (bf16[64]{0:T(256)(128)(2,1)S(1)}, bf16[64]{0:T(256)(128)(2,1)}, u32[]{:S(2)}) copy-start(bf16[64]{0:T(256)(128)(2,1)} %param.22) | copy-start | bytes 388
  11.9 62.4 %copy-start.55 = (bf16[64]{0:T(256)(128)(2,1)S(1)}, bf16[64]{0:T(256)(128)(2,1)}, u32[]{:S(2)}) copy-start(bf16[64]{0:T(256)(128)(2,1)} %param.23) | copy-start | bytes 388
  11.9 62.4 %copy-start.56 = (bf16[64]{0:T(256)(128)(2,1)S(1)}, bf16[64]{0:T(256)(128)(2,1)}, u32[]{:S(2)}) copy-start(bf16[64]{0:T(256)(128)(2,1)} %param.24) | copy-start | bytes 388
  12.3 128.9 %copy-start.57 = (s32[2]{0:T(128)S(1)}, s32[2]{0:T(128)}, u32[]{:S(2)}) copy-start(s32[2]{0:T(128)} %param.18) | copy-start | bytes 28
  62.6 139.6 %all-gather.13.cloned.1.call-start = ((), (), s32[]{:S(2)}) async-start(), calls=%async_computation.14 | async-start | bytes 1310720 | tf_op jit(solution)/shard_map/all_gather | solution.py:99
  63.4 189.8 %reduce-scatter.11.cloned.1.call-start = ((), (), s32[]{:S(2)}) async-start(), calls=%async_computation.15 | async-start | bytes 4718592 | tf_op jit(solution)/shard_map/reduce_scatter | solution.py:145
  141.1 13.0 copy-start.30
  143.0 43.5 %copy-start.40 = (f32[256,1]{0,1:T(1,128)}, f32[256,1]{0,1:T(1,128)S(1)}, u32[]{:S(2)}) copy-start(f32[256,1]{0,1:T(1,128)S(1)} %get-tuple-element.77) | copy-start | bytes 3076
  143.0 44.8 %copy-start.38 = (f32[256,1]{0,1:T(1,128)}, f32[256,1]{0,1:T(1,128)S(1)}, u32[]{:S(2)}) copy-start(f32[256,1]{0,1:T(1,128)S(1)} %get-tuple-element.78) | copy-start | bytes 3076
  147.4 6.7 copy-start.47
  170.0 6.1 copy-start.32
  170.0 6.1 copy-start.34
  170.4 28.0 %copy-start.17 = (bf16[2,2,8,64,128]{4,3,2,1,0:T(8,128)(2,1)}, bf16[2,2,8,64,128]{4,3,2,1,0:T(8,128)(2,1)S(1)}, u32[]{:S(2)}) copy-start(bf16[2,2,8,64,128]{4,3,2,1,0:T(8,128)(2,1)S(1)} %copy.216) | copy-start | bytes 1572868
  185.1 2.8 copy-start.24
  189.8 5.8 copy-start.19
  195.6 6.0 copy-start.42
  202.2 4.7 copy-start.13
  202.2 51.0 %copy-start.1 = (bf16[2,64,2048]{2,1,0:T(8,128)(2,1)S(1)}, bf16[2,64,2048]{2,1,0:T(8,128)(2,1)}, u32[]{:S(2)}) copy-start(bf16[2,64,2048]{2,1,0:T(8,128)(2,1)} %param.17) | copy-start | bytes 1572868
  206.9 196.3 %all-gather.15.cloned.1.call-start = ((), (), s32[]{:S(2)}) async-start(), calls=%async_computation.16 | async-start | bytes 17301504 | tf_op jit(solution)/shard_map/all_gather | solution.py:154
  254.5 9.0 copy-start.44
  256.6 262.4 %all-gather.17.cloned.1.call-start = ((), (), s32[]{:S(2)}) async-start(), calls=%async_computation.18 | async-start | bytes 17301504 | tf_op jit(solution)/shard_map/all_gather | solution.py:157
  263.6 6.1 copy-start.46
  265.0 81.8 %all-to-all-start.1 = ((bf16[8,256,512]{1,2,0:T(8,128)(2,1)}), bf16[8,256,512]{1,2,0:T(8,128)(2,1)}, u32[]{:S(2)}, u32[]{:S(2)}) async-start(bf16[8,256,512]{1,2,0:T(8,128)(2,1)} %bitcast.188), calls=%async_computation.2 | async-start | bytes 4194304 | tf_op jit(solution)/shard_map/all_to_all | solution.py:102
  269.4 402.5 %reduce-scatter.17.cloned.1.call-start = ((), (), s32[]{:S(2)}) async-start(), calls=%async_computation.20 | async-start | bytes 135168 | tf_op jit(solution)/shard_map/reduce_scatter | solution.py:184
  519.0 20.8 %copy-start.5 = (bf16[128,2048]{1,0:T(8,128)(2,1)S(1)}, bf16[128,2048]{1,0:T(8,128)(2,1)}, u32[]{:S(2)}) copy-start(bf16[128,2048]{1,0:T(8,128)(2,1)} %multiply_convert_fusion.6) | copy-start | bytes 1572868
  539.7 576.7 %reduce-scatter.15.cloned.1.call-start = ((), (), s32[]{:S(2)}) async-start(), calls=%async_computation.19 | async-start | bytes 17301504 | tf_op jit(solution)/shard_map/reduce_scatter | solution.py:180
  672.6 443.9 %copy-start.50 = (f32[128]{0:T(128)}, f32[128]{0:T(128)S(1)}, u32[]{:S(2)}) copy-start(f32[128]{0:T(128)S(1)} %get-tuple-element.62) | copy-start | bytes 1540
  744.6 2.0 copy-start.16
  760.6 355.8 %copy-start.31 = (bf16[2048,12]{0,1:T(8,128)(2,1)S(1)}, bf16[2048,12]{0,1:T(8,128)(2,1)}, u32[]{:S(2)}) copy-start(bf16[2048,12]{0,1:T(8,128)(2,1)} %copy-done.30) | copy-start | bytes 147460
  760.7 355.8 %copy-start.36 = (f32[128,8]{0,1:T(8,128)S(1)}, f32[128,8]{0,1:T(8,128)}, u32[]{:S(2)}) copy-start(f32[128,8]{0,1:T(8,128)} %reduce-scatter.17.cloned.1.call-done) | copy-start | bytes 12292
  760.7 355.8 %copy-start.37 = (pred[128,8]{0,1:T(8,128)(4,1)S(1)}, pred[128,8]{0,1:T(8,128)(4,1)}, u32[]{:S(2)}) copy-start(pred[128,8]{0,1:T(8,128)(4,1)} %fusion.33) | copy-start | bytes 3076
  760.7 355.8 %copy-start.45 = (f32[128]{0:T(128)S(1)}, f32[128]{0:T(128)}, u32[]{:S(2)}) copy-start(f32[128]{0:T(128)} %copy-done.44) | copy-start | bytes 1540
  760.7 410.3 %all-gather.19.cloned.1.call-start = ((), (), s32[]{:S(2)}) async-start(), calls=%async_computation.21 | async-start | bytes 4718592 | tf_op jit(solution)/shard_map/all_gather | solution.py:203
  1122.2 217.7 %reduce-scatter.21.cloned.1.call-start = ((), (), s32[]{:S(2)}) async-start(), calls=%async_computation.23 | async-start | bytes 3932160 | tf_op jit(solution)/shard_map/reduce_scatter | solution.py:235
  1175.6 7.4 copy-start.43
  1177.6 5.5 copy-start.11
  1177.6 5.5 copy-start.18
  1200.0 7.2 copy-start.39
  1202.5 3.9 copy-start.9
  1202.5 4.7 copy-start.3
  1208.8 19.8 %copy-start.35 = (f32[1,1024]{1,0:T(1,128)S(1)}, f32[1,1024]{1,0:T(1,128)}, u32[]{:S(2)}) copy-start(f32[1,1024]{1,0:T(1,128)} %copy-done.34) | copy-start | bytes 12292
  1208.8 21.8 %copy-start.33 = (f32[1,1024]{1,0:T(1,128)S(1)}, f32[1,1024]{1,0:T(1,128)}, u32[]{:S(2)}) copy-start(f32[1,1024]{1,0:T(1,128)} %copy-done.32) | copy-start | bytes 12292
  1212.4 19.9 %copy-start.48 = (f32[1024]{0:T(1024)S(1)}, f32[1024]{0:T(1024)}, u32[]{:S(2)}) copy-start(f32[1024]{0:T(1024)} %copy-done.47) | copy-start | bytes 12292
  1228.6 3.7 copy-start.10
  1228.6 3.7 copy-start.28
  1230.6 7.3 copy-start.25
  1232.3 5.6 copy-start.27
  1232.3 5.6 copy-start.14
  1237.9 4.7 copy-start.26
  1237.9 136.4 %reduce-scatter.23.cloned.1.call-start = ((), (), s32[]{:S(2)}) async-start(), calls=%async_computation.24 | async-start | bytes 1310720 | tf_op jit(solution)/shard_map/reduce_scatter | solution.py:206
  1242.5 145.1 %reduce-scatter.19.cloned.1.call-start = ((), (), s32[]{:S(2)}) async-start(), calls=%async_computation.22 | async-start | bytes 4718592 | tf_op jit(solution)/shard_map/reduce_scatter | solution.py:233
  1250.4 495.1 %reduce-scatter.13.cloned.1.call-start = ((), (), s32[]{:S(2)}) async-start(), calls=%async_computation.17 | async-start | bytes 17301504 | tf_op jit(solution)/shard_map/reduce_scatter | solution.py:169
  1275.5 64.4 %all-to-all-start.3 = ((bf16[8,256,512]{2,1,0:T(8,128)(2,1)}), bf16[8,256,512]{2,1,0:T(8,128)(2,1)}, u32[]{:S(2)}, u32[]{:S(2)}) async-start(bf16[8,256,512]{2,1,0:T(8,128)(2,1)} %bitcast.208), calls=%async_computation.10 | async-start | bytes 4194304 | tf_op jit(solution)/shard_map/all_to_all | solution.py:185
  1339.9 37.4 %all-to-all-start.2 = ((bf16[8,64,768]{2,1,0:T(8,128)(2,1)}), bf16[8,64,768]{2,1,0:T(8,128)(2,1)S(1)}, u32[]{:S(2)}, u32[]{:S(2)}) async-start(bf16[8,64,768]{2,1,0:T(8,128)(2,1)} %reduce-scatter.21.cloned.1.call-done), calls=%async_computation.8 | async-start | bytes 1572864 | tf_op jit(solution)/shard_map/all_to_all | solution.py:236
  1343.5 12.4 copy-start.51
  1343.5 540.5 %reduce-scatter.25.cloned.1.call-start = ((), (), s32[]{:S(2)}) async-start(), calls=%async_computation.25 | async-start | bytes 1081344
  1384.1 361.4 %copy-start.6 = (bf16[128,2048]{1,0:T(8,128)(2,1)S(1)}, bf16[128,2048]{1,0:T(8,128)(2,1)}, u32[]{:S(2)}) copy-start(bf16[128,2048]{1,0:T(8,128)(2,1)} %reduce-scatter.11.cloned.1.call-done) | copy-start | bytes 1572868
  1384.1 361.4 %copy-start.8 = (bf16[2,64,2048]{2,1,0:T(8,128)(2,1)S(1)}, bf16[2,64,2048]{2,1,0:T(8,128)(2,1)}, u32[]{:S(2)}) copy-start(bf16[2,64,2048]{2,1,0:T(8,128)(2,1)} %param.33) | copy-start | bytes 1572868
  (11 other events, 15.0 us)
Sparse Core Ops, SparseCore 0:
  9.6 66.5 all-gather.8
  78.1 43.6 all-gather.10
  123.6 26.6 all-gather.12
  207.0 46.1 reduce-scatter.10
  256.7 146.4 all-gather.14
  405.9 113.0 all-gather.16
  539.9 131.9 reduce-scatter.16
  760.8 355.6 reduce-scatter.14
  1122.4 48.6 all-gather.18
  1238.0 42.0 reduce-scatter.20
  1283.3 27.7 reduce-scatter.22
  1313.2 66.1 reduce-scatter.18
  1381.7 363.7 reduce-scatter.12
  1747.6 136.3 reduce-scatter.24
where the time goes:
time: 1900 us
  waiting for transfers between devices  1360 us (72%)
  blocking collectives  218 us (11%)
  matrix products  138 us (7%)
  local copies, waits for them, and re-layouts  89.4 us (5%)
  other arithmetic  56.6 us (3%)
    reduce_scatter x1, waiting for transfers between devices, shards(): lax.psum_scatter(grad_normed, every, scatter_dimension=0, tiled=True)  356 us
    reduce_scatter x1, waiting for transfers between devices, shards(): mixture = lax.psum_scatter(mixture, every, scatter_dimension=0, tiled=True)  355 us
    unnamed x15, waiting for transfers between devices  137 us
    reduce_scatter x1, waiting for transfers between devices, shards(): lax.psum_scatter(grad_gates, every, scatter_dimension=0, tiled=True)  131 us
    all_gather x1, waiting for transfers between devices, shards(): dy_all = lax.all_gather(dy_own, every, axis=0, tiled=True)  101 us
    all_to_all x1, waiting for transfers between devices, shards(): lax.all_to_all(gu_cut, 'seq', 0, 0, tiled=True)  76.5 us
    all_gather x1, blocking collectives, shards(): small_all = lax.all_gather(small, every, axis=0, tiled=True)  66.6 us
    all_gather x1, blocking collectives, shards(): gates_all = lax.all_gather(gates, every, axis=0, tiled=True)  64.6 us
  transfers between devices with their start and end apart: 17, of which 11 were waited for; matrix products, arithmetic and copies ran while one was open for 9% of the time, Pallas kernels for 0%

commit v1 on v0

--- a/solution.py
+++ b/solution.py
@@ -200,7 +200,14 @@
     grad_resid, gain_mlp_terms = rms_back(residual, scale_r, gain_mlp, grad_normed)
     grad_residual = dy_own.astype(F32) + grad_resid
     grad_o = grad_residual.astype(BF)
-    grad_o_col = lax.all_gather(grad_o, "seq", axis=0, tiled=True)
+    ways, here = (lax.axis_size("seq"), lax.axis_index("seq"))
+    grad_o_col, reach = (grad_o, 1)
+    while reach < ways:
+        theirs = lax.ppermute(grad_o_col, "seq", [(d, d ^ reach) for d in range(ways)])
+        mine_first = jnp.concatenate([grad_o_col, theirs], axis=0)
+        theirs_first = jnp.concatenate([theirs, grad_o_col], axis=0)
+        grad_o_col = jnp.where(here & reach == 0, mine_first, theirs_first)
+        reach = 2 * reach
     grad_mixed = by_row(dot_t(grad_o_col, w_o).astype(BF))
     grad_w_o = t_dot(mixed, grad_o_col).astype(BF)
     grad_w_o = lax.psum_scatter(grad_w_o, "batch", scatter_dimension=0, tiled=True).astype(F32)

time: 1900 us -> 1990 us (1.047)
  waiting for transfers between devices: 1360 us -> 1430 us
    ppermute x0 -> x3, waiting for transfers between devices: none -> 117 us  [shards(): lax.ppermute(grad_o_col, 'seq', [(d, d ^ reach) for d in range(ways)])]
    all_gather x1 -> x0, waiting for transfers between devices: 48.6 us -> none  [shards(): grad_o_col = lax.all_gather(grad_o, 'seq', axis=0, tiled=True)]
    unnamed x15 -> x14, waiting for transfers between devices: 137 us -> 137 us
  transfers between devices with their start and end apart: 17 -> 19, of which waited for: 11 -> 12; matrix products, arithmetic and copies ran while one was open for 9% -> 8% of each run, Pallas kernels for 0% -> 0%
where the time goes in v1:
time: 1990 us; the launch traced here: 1980 us
  waiting for transfers between devices  1430 us (72%)
  blocking collectives  220 us (11%)
  matrix products  141 us (7%)
  local copies, waits for them, and re-layouts  89.3 us (4%)
  other arithmetic  63.9 us (3%)
    reduce_scatter x1, waiting for transfers between devices, shards(): lax.psum_scatter(grad_normed, every, scatter_dimension=0, tiled=True)  355 us
    reduce_scatter x1, waiting for transfers between devices, shards(): mixture = lax.psum_scatter(mixture, every, scatter_dimension=0, tiled=True)  353 us
    unnamed x14, waiting for transfers between devices  137 us
    reduce_scatter x1, waiting for transfers between devices, shards(): lax.psum_scatter(grad_gates, every, scatter_dimension=0, tiled=True)  131 us
    ppermute x3, waiting for transfers between devices, shards(): lax.ppermute(grad_o_col, 'seq', [(d, d ^ reach) for d in range(ways)])  117 us
    all_gather x1, waiting for transfers between devices, shards(): dy_all = lax.all_gather(dy_own, every, axis=0, tiled=True)  101 us
    all_to_all x1, waiting for transfers between devices, shards(): lax.all_to_all(gu_cut, 'seq', 0, 0, tiled=True)  76.5 us
    all_gather x1, blocking collectives, shards(): small_all = lax.all_gather(small, every, axis=0, tiled=True)  66.6 us
  transfers between devices with their start and end apart: 19, of which 12 were waited for; matrix products, arithmetic and copies ran while one was open for 8% of the time, Pallas kernels for 0%

profile of v1, /device:TPU:0, one launch (start us, length us, event | category | flops | bytes accessed | tf_op | source)
XLA Modules:
  0.0 1979.0 jit_solution(6593629117438228304)
XLA Ops:
  15.1 47.5 %all_to_all.20 = bf16[8,64,768]{2,1,0:T(8,128)(2,1)} all-to-all(bf16[8,64,768]{2,1,0:T(8,128)(2,1)S(1)} %reshape.364), channel_id=1, replica_groups=mesh['seq'=8,'batch'=4] {'seq'}, dimensions={0} | all-to-all | bytes 1572864 | tf_op jit(solution)/shard_map/all_to_all | solution.py:97
  63.6 10.6 all-gather
  74.4 66.6 %all-gather.1 = bf16[32,64,12]{1,2,0:T(8,128)(2,1)S(1)} all-gather(bf16[1,64,12]{1,2,0:T(8,128)(2,1)S(1)} %bitcast.248), channel_id=1, replica_groups=mesh['seq'=8,'batch'=4] {'seq','batch'}, dimensions={0}, use_global_device_ids=true | all-gather | bytes 50688 | tf_op jit(solution)/shard_map/all_gather | solution.py:89
  144.3 3.1 fusion.1
  147.4 6.7 fusion.15
  155.8 14.4 psum.14
  170.7 3.0 slice_multiply_fusion.1
  173.8 2.5 copy.211
  176.3 2.7 reshape.366
  179.0 2.3 copy.212
  182.7 2.7 reshape.368
  190.1 5.8 fusion.57
  195.9 2.8 fusion.10
  202.5 4.6 convolution_convert_fusion.2
  207.2 46.3 %reduce-scatter.11.cloned.1.call-done = bf16[128,2048]{1,0:T(8,128)(2,1)} async-done(((bf16[1024,2048]{1,0:T(8,128)(2,1)}), bf16[128,2048]{1,0:T(8,128)(2,1)}) %reduce-scatter.11.cloned.1.call-update) | async-done | bytes 524304 | tf_op jit(solution)/shard_map/reduce_scatter | solution.py:145
  254.8 2.0 multiply_convert_fusion.6
  257.5 2.3 copy.219
  259.7 2.3 copy.220
  265.3 4.3 all-to-all-start.1
  270.6 76.5 %all-to-all-done.1 = bf16[8,256,512]{1,2,0:T(8,128)(2,1)} async-done(((bf16[8,256,512]{1,2,0:T(8,128)(2,1)}), bf16[8,256,512]{1,2,0:T(8,128)(2,1)}, u32[]{:S(2)}, u32[]{:S(2)}) %all-to-all-start.1) | async-done | bytes 2097184 | tf_op jit(solution)/shard_map/all_to_all | solution.py:102
  347.1 3.9 copy.222
  351.0 52.5 %all-gather.14.cloned.1.call-done = bf16[4096,2048]{1,0:T(8,128)(2,1)} async-done(((bf16[128,2048]{1,0:T(8,128)(2,1)}), bf16[4096,2048]{1,0:T(8,128)(2,1)}) %all-gather.14.cloned.1.call-update) | async-done | bytes 16777232 | tf_op jit(solution)/shard_map/all_gather | solution.py:154
  403.5 15.1 fusion.60
  418.6 100.7 %all-gather.16.cloned.1.call-done = bf16[4096,2048]{1,0:T(8,128)(2,1)} async-done(((bf16[128,2048]{1,0:T(8,128)(2,1)}), bf16[4096,2048]{1,0:T(8,128)(2,1)}) %all-gather.16.cloned.1.call-update) | async-done | bytes 16777232 | tf_op jit(solution)/shard_map/all_gather | solution.py:157
  519.3 20.0 %bitcast_reduce_fusion = (f32[4096,2]{0,1:T(2,128)S(1)}, bf16[4096,256]{0,1:T(8,128)(2,1)}, f32[4096,256]{0,1:T(8,128)}) fusion(f32[4096,512]{0,1:T(8,128)} %fusion.60, bf16[4096,2048]{1,0:T(8,128)(2,1)} %all-gather.16.cloned.1.call-done, bf16[256,2048]{1,0:T(8,128)(2,1)S(1)} %bitcast.181), kind=kOutput, calls=%fused_computation.14 | convolution fusion | flops 4304396288 | bytes 32538624 | tf_op jit(solution)/shard_map/dot_general | solution.py:19
  541.1 131.0 %reduce-scatter.17.cloned.1.call-done = f32[128,8]{0,1:T(8,128)} async-done(((f32[4096,8]{0,1:T(8,128)}), f32[128,8]{0,1:T(8,128)}) %reduce-scatter.17.cloned.1.call-update) | async-done | bytes 4112 | tf_op jit(solution)/shard_map/reduce_scatter | solution.py:184
  672.9 64.2 %all_gather.30 = f32[4096,8]{0,1:T(8,128)S(1)} all-gather(f32[128,8]{0,1:T(8,128)S(1)} %get-tuple-element.63), channel_id=1, replica_groups=mesh['seq'=8,'batch'=4] {'seq','batch'}, dimensions={0}, use_global_device_ids=true | all-gather | bytes 135168 | tf_op jit(solution)/shard_map/all_gather | solution.py:155
  737.1 7.3 multiply_convert_fusion.2
  746.4 14.1 convolution_convert_fusion
  761.0 355.3 %reduce-scatter.15.cloned.1.call-done = bf16[128,2048]{1,0:T(8,128)(2,1)} async-done(((bf16[4096,2048]{1,0:T(8,128)(2,1)}), bf16[128,2048]{1,0:T(8,128)(2,1)}) %reduce-scatter.15.cloned.1.call-update) | async-done | bytes 524304 | tf_op jit(solution)/shard_map/reduce_scatter | solution.py:180
  1116.4 2.3 multiply_reduce_fusion
  1119.6 2.5 fusion.51
  1122.1 2.2 collective-permute-done
  1124.3 2.9 maximum_select_fusion.2
  1129.0 23.8 %collective-permute-done.1 = bf16[256,2048]{1,0:T(8,128)(2,1)} collective-permute-done((bf16[256,2048]{1,0:T(8,128)(2,1)}, bf16[256,2048]{1,0:T(8,128)(2,1)}, u32[]{:S(2)}, u32[]{:S(2)}) %collective-permute-start.1) | collective-permute-done | bytes 1048608 | tf_op jit(solution)/shard_map/ppermute | solution.py:206
  1152.8 4.6 maximum_select_fusion.1
  1157.3 3.0 collective-permute-start.2
  1160.3 90.7 %collective-permute-done.2 = bf16[512,2048]{1,0:T(8,128)(2,1)} collective-permute-done((bf16[512,2048]{1,0:T(8,128)(2,1)}, bf16[512,2048]{1,0:T(8,128)(2,1)}, u32[]{:S(2)}, u32[]{:S(2)}) %collective-permute-start.2) | collective-permute-done | bytes 2097184 | tf_op jit(solution)/shard_map/ppermute | solution.py:206
  1251.0 5.9 convolution_convert_fusion.8
  1262.1 2.3 convolution_convert_fusion.7
  1267.4 2.0 convolution_multiply_fusion.1
  1270.9 2.0 copy.241
  1272.9 4.2 multiply_subtract_fusion.1
  1281.4 2.5 copy.238
  1291.2 2.5 copy.237
  1295.1 16.9 psum.15
  1315.7 5.5 convolution_convert_fusion.4
  1321.4 5.9 convolution_convert_fusion.6
  1327.5 7.7 convolution_convert_fusion.3
  1335.3 9.9 convolution_convert_fusion.1
  1345.3 14.7 convolution_convert_fusion.5
  1360.0 4.3 all-to-all-start.3
  1364.6 62.0 %all-to-all-done.3 = bf16[8,256,512]{2,1,0:T(8,128)(2,1)} async-done(((bf16[8,256,512]{2,1,0:T(8,128)(2,1)}), bf16[8,256,512]{2,1,0:T(8,128)(2,1)}, u32[]{:S(2)}, u32[]{:S(2)}) %all-to-all-start.3) | async-done | bytes 2097184 | tf_op jit(solution)/shard_map/all_to_all | solution.py:185
  1426.6 3.5 all-to-all-start.2
  1430.5 12.4 fusion.61
  1443.2 5.4 reshape.395
  1448.7 4.7 copy.284
  1453.3 2.4 fusion.52
  1455.7 2.7 squeeze.39
  1458.4 2.7 squeeze.38
  1464.8 4.6 fusion.53
  1476.1 352.6 %reduce-scatter.13.cloned.1.call-done = bf16[128,2048]{1,0:T(8,128)(2,1)} async-done(((bf16[4096,2048]{1,0:T(8,128)(2,1)}), bf16[128,2048]{1,0:T(8,128)(2,1)}) %reduce-scatter.13.cloned.1.call-update) | async-done | bytes 524304 | tf_op jit(solution)/shard_map/reduce_scatter | solution.py:169
  1828.7 3.3 fusion.19
  1832.0 135.2 %reduce-scatter.25.cloned.1.call-done = f32[64,12]{1,0:T(8,128)} async-done(((f32[2048,12]{1,0:T(8,128)}), f32[64,12]{1,0:T(8,128)}) %reduce-scatter.25.cloned.1.call-update) | async-done | bytes 3088
  (250 shorter events, 80.3 us)
Async XLA Ops:
  7.2 512.1 %copy-start = (bf16[2,128,2048]{2,1,0:T(8,128)(2,1)S(1)}, bf16[2,128,2048]{2,1,0:T(8,128)(2,1)}, u32[]{:S(2)}) copy-start(bf16[2,128,2048]{2,1,0:T(8,128)(2,1)} %param.32) | copy-start | bytes 3145732
  7.2 137.1 %all-gather.8.cloned.1.call-start = ((), (), s32[]{:S(2)}) async-start(), calls=%async_computation.12 | async-start | bytes 4718592 | tf_op jit(solution)/shard_map/all_gather | solution.py:105
  7.9 139.5 %all-gather.10.cloned.1.call-start = ((), (), s32[]{:S(2)}) async-start(), calls=%async_computation.13 | async-start | bytes 3932160 | tf_op jit(solution)/shard_map/all_gather | solution.py:98
  11.8 51.8 %copy-start.52 = (s32[2,64]{1,0:T(2,128)S(1)}, s32[2,64]{1,0:T(2,128)}, u32[]{:S(2)}) copy-start(s32[2,64]{1,0:T(2,128)} %param.19) | copy-start | bytes 1540
  11.8 62.5 %copy-start.49 = (bf16[64,8]{0,1:T(8,128)(2,1)S(1)}, bf16[64,8]{0,1:T(8,128)(2,1)}, u32[]{:S(2)}) copy-start(bf16[64,8]{0,1:T(8,128)(2,1)} %param.29) | copy-start | bytes 3076
  11.8 62.4 %copy-start.53 = (bf16[64]{0:T(256)(128)(2,1)S(1)}, bf16[64]{0:T(256)(128)(2,1)}, u32[]{:S(2)}) copy-start(bf16[64]{0:T(256)(128)(2,1)} %param.21) | copy-start | bytes 388
  11.9 62.4 %copy-start.54 = (bf16[64]{0:T(256)(128)(2,1)S(1)}, bf16[64]{0:T(256)(128)(2,1)}, u32[]{:S(2)}) copy-start(bf16[64]{0:T(256)(128)(2,1)} %param.22) | copy-start | bytes 388
  11.9 62.4 %copy-start.55 = (bf16[64]{0:T(256)(128)(2,1)S(1)}, bf16[64]{0:T(256)(128)(2,1)}, u32[]{:S(2)}) copy-start(bf16[64]{0:T(256)(128)(2,1)} %param.23) | copy-start | bytes 388
  11.9 62.4 %copy-start.56 = (bf16[64]{0:T(256)(128)(2,1)S(1)}, bf16[64]{0:T(256)(128)(2,1)}, u32[]{:S(2)}) copy-start(bf16[64]{0:T(256)(128)(2,1)} %param.24) | copy-start | bytes 388
  12.3 128.9 %copy-start.57 = (s32[2]{0:T(128)S(1)}, s32[2]{0:T(128)}, u32[]{:S(2)}) copy-start(s32[2]{0:T(128)} %param.18) | copy-start | bytes 28
  62.6 139.9 %all-gather.12.cloned.1.call-start = ((), (), s32[]{:S(2)}) async-start(), calls=%async_computation.14 | async-start | bytes 1310720 | tf_op jit(solution)/shard_map/all_gather | solution.py:99
  63.4 190.1 %reduce-scatter.11.cloned.1.call-start = ((), (), s32[]{:S(2)}) async-start(), calls=%async_computation.15 | async-start | bytes 4718592 | tf_op jit(solution)/shard_map/reduce_scatter | solution.py:145
  141.1 13.0 copy-start.30
  143.0 43.8 %copy-start.40 = (f32[256,1]{0,1:T(1,128)}, f32[256,1]{0,1:T(1,128)S(1)}, u32[]{:S(2)}) copy-start(f32[256,1]{0,1:T(1,128)S(1)} %get-tuple-element.77) | copy-start | bytes 3076
  143.0 45.1 %copy-start.38 = (f32[256,1]{0,1:T(1,128)}, f32[256,1]{0,1:T(1,128)S(1)}, u32[]{:S(2)}) copy-start(f32[256,1]{0,1:T(1,128)S(1)} %get-tuple-element.78) | copy-start | bytes 3076
  147.4 6.7 copy-start.47
  170.2 6.1 copy-start.32
  170.3 6.1 copy-start.34
  170.7 28.0 %copy-start.17 = (bf16[2,2,8,64,128]{4,3,2,1,0:T(8,128)(2,1)}, bf16[2,2,8,64,128]{4,3,2,1,0:T(8,128)(2,1)S(1)}, u32[]{:S(2)}) copy-start(bf16[2,2,8,64,128]{4,3,2,1,0:T(8,128)(2,1)S(1)} %copy.216) | copy-start | bytes 1572868
  190.1 5.8 copy-start.19
  195.9 6.0 copy-start.42
  202.5 4.7 copy-start.13
  202.5 51.0 %copy-start.1 = (bf16[2,64,2048]{2,1,0:T(8,128)(2,1)S(1)}, bf16[2,64,2048]{2,1,0:T(8,128)(2,1)}, u32[]{:S(2)}) copy-start(bf16[2,64,2048]{2,1,0:T(8,128)(2,1)} %param.17) | copy-start | bytes 1572868
  207.2 196.3 %all-gather.14.cloned.1.call-start = ((), (), s32[]{:S(2)}) async-start(), calls=%async_computation.16 | async-start | bytes 17301504 | tf_op jit(solution)/shard_map/all_gather | solution.py:154
  254.8 9.0 copy-start.44
  256.9 262.4 %all-gather.16.cloned.1.call-start = ((), (), s32[]{:S(2)}) async-start(), calls=%async_computation.18 | async-start | bytes 17301504 | tf_op jit(solution)/shard_map/all_gather | solution.py:157
  263.9 6.1 copy-start.46
  265.3 81.8 %all-to-all-start.1 = ((bf16[8,256,512]{1,2,0:T(8,128)(2,1)}), bf16[8,256,512]{1,2,0:T(8,128)(2,1)}, u32[]{:S(2)}, u32[]{:S(2)}) async-start(bf16[8,256,512]{1,2,0:T(8,128)(2,1)} %bitcast.186), calls=%async_computation.2 | async-start | bytes 4194304 | tf_op jit(solution)/shard_map/all_to_all | solution.py:102
  269.7 402.5 %reduce-scatter.17.cloned.1.call-start = ((), (), s32[]{:S(2)}) async-start(), calls=%async_computation.20 | async-start | bytes 135168 | tf_op jit(solution)/shard_map/reduce_scatter | solution.py:184
  519.3 20.8 %copy-start.5 = (bf16[128,2048]{1,0:T(8,128)(2,1)S(1)}, bf16[128,2048]{1,0:T(8,128)(2,1)}, u32[]{:S(2)}) copy-start(bf16[128,2048]{1,0:T(8,128)(2,1)} %multiply_convert_fusion.6) | copy-start | bytes 1572868
  540.0 576.3 %reduce-scatter.15.cloned.1.call-start = ((), (), s32[]{:S(2)}) async-start(), calls=%async_computation.19 | async-start | bytes 17301504 | tf_op jit(solution)/shard_map/reduce_scatter | solution.py:180
  672.9 443.5 %copy-start.50 = (f32[128]{0:T(128)}, f32[128]{0:T(128)S(1)}, u32[]{:S(2)}) copy-start(f32[128]{0:T(128)S(1)} %get-tuple-element.62) | copy-start | bytes 1540
  760.5 355.8 %copy-start.31 = (bf16[2048,12]{0,1:T(8,128)(2,1)S(1)}, bf16[2048,12]{0,1:T(8,128)(2,1)}, u32[]{:S(2)}) copy-start(bf16[2048,12]{0,1:T(8,128)(2,1)} %copy-done.30) | copy-start | bytes 147460
  760.5 355.8 %copy-start.36 = (f32[128,8]{0,1:T(8,128)S(1)}, f32[128,8]{0,1:T(8,128)}, u32[]{:S(2)}) copy-start(f32[128,8]{0,1:T(8,128)} %reduce-scatter.17.cloned.1.call-done) | copy-start | bytes 12292
  760.5 355.8 %copy-start.37 = (pred[128,8]{0,1:T(8,128)(4,1)S(1)}, pred[128,8]{0,1:T(8,128)(4,1)}, u32[]{:S(2)}) copy-start(pred[128,8]{0,1:T(8,128)(4,1)} %fusion.33) | copy-start | bytes 3076
  760.5 355.8 %copy-start.45 = (f32[128]{0:T(128)S(1)}, f32[128]{0:T(128)}, u32[]{:S(2)}) copy-start(f32[128]{0:T(128)} %copy-done.44) | copy-start | bytes 1540
  760.5 666.1 %reduce-scatter.21.cloned.1.call-start = ((), (), s32[]{:S(2)}) async-start(), calls=%async_computation.22 | async-start | bytes 3932160 | tf_op jit(solution)/shard_map/reduce_scatter | solution.py:242
  1122.1 2.3 collective-permute-start
  1127.3 25.5 %collective-permute-start.1 = (bf16[256,2048]{1,0:T(8,128)(2,1)}, bf16[256,2048]{1,0:T(8,128)(2,1)}, u32[]{:S(2)}, u32[]{:S(2)}) collective-permute-start(bf16[256,2048]{1,0:T(8,128)(2,1)} %maximum_select_fusion.2), channel_id=1, source_target_pairs={{0,8},{4,12},{8,0},{12,4},{16,24},{20,28},{24,16},{28,20},{1,9},{5... | collective-permute-start | bytes 3145736 | tf_op jit(solution)/shard_map/ppermute | solution.py:206
  1157.3 93.7 %collective-permute-start.2 = (bf16[512,2048]{1,0:T(8,128)(2,1)}, bf16[512,2048]{1,0:T(8,128)(2,1)}, u32[]{:S(2)}, u32[]{:S(2)}) collective-permute-start(bf16[512,2048]{1,0:T(8,128)(2,1)} %maximum_select_fusion.1), channel_id=1, source_target_pairs={{0,16},{4,20},{8,24},{12,28},{16,0},{20,4},{24,8},{28,12},{1,17},{... | collective-permute-start | bytes 6291464 | tf_op jit(solution)/shard_map/ppermute | solution.py:206
  1257.0 7.4 copy-start.43
  1258.9 5.5 copy-start.11
  1258.9 5.5 copy-start.18
  1281.4 7.2 copy-start.39
  1284.0 3.9 copy-start.9
  1284.0 4.7 copy-start.3
  1290.1 22.0 %copy-start.35 = (f32[1,1024]{1,0:T(1,128)S(1)}, f32[1,1024]{1,0:T(1,128)}, u32[]{:S(2)}) copy-start(f32[1,1024]{1,0:T(1,128)} %copy-done.34) | copy-start | bytes 12292
  1290.1 23.9 %copy-start.33 = (f32[1,1024]{1,0:T(1,128)S(1)}, f32[1,1024]{1,0:T(1,128)}, u32[]{:S(2)}) copy-start(f32[1,1024]{1,0:T(1,128)} %copy-done.32) | copy-start | bytes 12292
  1293.7 22.0 %copy-start.48 = (f32[1024]{0:T(1024)S(1)}, f32[1024]{0:T(1024)}, u32[]{:S(2)}) copy-start(f32[1024]{0:T(1024)} %copy-done.47) | copy-start | bytes 12292
  1312.0 3.7 copy-start.10
  1312.0 3.7 copy-start.28
  1314.0 7.3 copy-start.25
  1315.7 5.6 copy-start.27
  1315.7 5.6 copy-start.14
  1321.3 6.2 copy-start.26
  1321.3 139.8 %reduce-scatter.23.cloned.1.call-start = ((), (), s32[]{:S(2)}) async-start(), calls=%async_computation.23 | async-start | bytes 1310720 | tf_op jit(solution)/shard_map/reduce_scatter | solution.py:213
  1327.3 145.9 %reduce-scatter.19.cloned.1.call-start = ((), (), s32[]{:S(2)}) async-start(), calls=%async_computation.21 | async-start | bytes 4718592 | tf_op jit(solution)/shard_map/reduce_scatter | solution.py:240
  1335.3 493.4 %reduce-scatter.13.cloned.1.call-start = ((), (), s32[]{:S(2)}) async-start(), calls=%async_computation.17 | async-start | bytes 17301504 | tf_op jit(solution)/shard_map/reduce_scatter | solution.py:169
  1360.0 66.6 %all-to-all-start.3 = ((bf16[8,256,512]{2,1,0:T(8,128)(2,1)}), bf16[8,256,512]{2,1,0:T(8,128)(2,1)}, u32[]{:S(2)}, u32[]{:S(2)}) async-start(bf16[8,256,512]{2,1,0:T(8,128)(2,1)} %bitcast.206), calls=%async_computation.10 | async-start | bytes 4194304 | tf_op jit(solution)/shard_map/all_to_all | solution.py:185
  1426.6 36.3 %all-to-all-start.2 = ((bf16[8,64,768]{2,1,0:T(8,128)(2,1)}), bf16[8,64,768]{2,1,0:T(8,128)(2,1)S(1)}, u32[]{:S(2)}, u32[]{:S(2)}) async-start(bf16[8,64,768]{2,1,0:T(8,128)(2,1)} %reduce-scatter.21.cloned.1.call-done), calls=%async_computation.8 | async-start | bytes 1572864 | tf_op jit(solution)/shard_map/all_to_all | solution.py:243
  1430.2 12.7 copy-start.51
  1430.2 537.1 %reduce-scatter.25.cloned.1.call-start = ((), (), s32[]{:S(2)}) async-start(), calls=%async_computation.24 | async-start | bytes 1081344
  1469.7 359.0 %copy-start.6 = (bf16[128,2048]{1,0:T(8,128)(2,1)S(1)}, bf16[128,2048]{1,0:T(8,128)(2,1)}, u32[]{:S(2)}) copy-start(bf16[128,2048]{1,0:T(8,128)(2,1)} %reduce-scatter.11.cloned.1.call-done) | copy-start | bytes 1572868
  1469.7 359.0 %copy-start.8 = (bf16[2,64,2048]{2,1,0:T(8,128)(2,1)S(1)}, bf16[2,64,2048]{2,1,0:T(8,128)(2,1)}, u32[]{:S(2)}) copy-start(bf16[2,64,2048]{2,1,0:T(8,128)(2,1)} %param.33) | copy-start | bytes 1572868
  (13 other events, 19.8 us)
Sparse Core Ops, SparseCore 0:
  9.6 66.5 all-gather.7
  78.1 43.6 all-gather.9
  123.6 26.6 all-gather.11
  207.3 46.1 reduce-scatter.10
  257.0 146.4 all-gather.13
  406.2 113.0 all-gather.15
  540.1 131.9 reduce-scatter.16
  760.7 355.6 reduce-scatter.14
  1321.4 41.6 reduce-scatter.20
  1366.1 27.7 reduce-scatter.22
  1396.2 66.1 reduce-scatter.18
  1464.5 364.1 reduce-scatter.12
  1830.9 136.2 reduce-scatter.24
